TPU v7x, 256 devices: a whole 4x4x8 slice. The times are simulated.
256 devices in a mesh: row: 8 (over x, y_lo), col: 32 (over y_hi, z, core).
Axes of the slice: x: 4, y: 4 (y_hi: 2, y_lo: 2; y = y_hi * 2 + y_lo), z: 8, core: 2. Of those that a mesh axis runs over, the one named last changes fastest.
Arguments:
- features: bfloat16 [32768, 512], P(('col', 'row')), may hold values from -6 to 6
- tile_vals: bfloat16 [8, 4096, 128, 128], P('row', 'col')
- tile_row: int32 [8, 4096], P('row', 'col'), may hold values from 0 to 31
- tile_col: int32 [8, 4096], P('row', 'col'), may hold values from 0 to 7
- tile_count: int32 [8, 32], P('row', 'col'), may hold values from 1 to 128, as said below
- node_type: int32 [32768], P(('row', 'col')), may hold values from 0 to 7
- type_gain: float32 [8, 512], replicated, may hold values from 0.1 to 1.9
- w_in: bfloat16 [512, 1024], replicated, may hold values from -0.25 to 0.25
- w_out: bfloat16 [1024, 512], replicated, may hold values from -0.1875 to 0.1875
- cotangent: bfloat16 [32768, 512], P(('row', 'col')), may hold values from -6 to 6
Outputs:
- mixed: bfloat16 [32768, 512], P(('row', 'col'))
- grad_x: float32 [32768, 512], P(('col', 'row'))
- grad_w_in: float32 [512, 1024], replicated
- grad_w_out: float32 [1024, 512], replicated
- grad_gain: float32 [8, 512], replicated
Inputs may be any that keep to these rules, and one draw needn't show every extreme that they name: Slots 0 to tile_count - 1 of a grid cell's list are live; some grid cell has all 128 slots live in every draw.
All inputs are finite; a program needn't handle non-finite values.
Results may differ from a plain program's by a relative error of at most 0.0056.
Values may be sent and summed in bfloat16 or wider, within the bound.
A program may use at most 128 MiB of HBM per device.

v0:
```python
import jax
import jax.numpy as jnp
from jax import lax
from jax.sharding import PartitionSpec as P

F = 512
TYPES = 8
TILE = 128


def sweep(weights_all, row_ids_all, col_ids_all, live_count, sources, target, forward, lower):
    span = target.shape[0]
    rounds = weights_all.shape[0] // 16

    def advance(block_index, totals):
        first_slot = block_index * 16
        weights_now = lax.dynamic_slice_in_dim(weights_all, first_slot, 16, 0)
        row_ids = lax.dynamic_slice_in_dim(row_ids_all, first_slot, 16, 0)
        col_ids = lax.dynamic_slice_in_dim(col_ids_all, first_slot, 16, 0)
        living = first_slot + jnp.arange(16, dtype=jnp.int32) < live_count
        if forward:
            pieces = sources[col_ids]
            product = jnp.einsum(
                "sab,sbf->saf", weights_now, pieces, preferred_element_type=jnp.float32
            )
            destination = row_ids - lower
        else:
            pieces = sources[row_ids]
            product = jnp.einsum(
                "sab,saf->sbf", weights_now, pieces, preferred_element_type=jnp.float32
            )
            destination = col_ids - lower
        inside = living & (destination >= 0) & (destination < span)
        product = jnp.where(inside[:, None, None], product, 0.0)
        placed = jnp.clip(destination, 0, span - 1)
        return totals.at[placed].add(product)

    return lax.fori_loop(0, rounds, advance, target)


def shards(
    features,
    tile_vals,
    tile_row,
    tile_col,
    tile_count,
    node_type,
    type_gain,
    w_in,
    w_out,
    cotangent,
):
    row_count = lax.axis_size("row")
    col_count = lax.axis_size("col")
    total_nodes = TILE * row_count * col_count
    weights_all = tile_vals[0]
    row_ids_all = tile_row[0]
    col_ids_all = tile_col[0]
    live_count = tile_count[0, 0]
    gathered = lax.all_gather(features, "row", axis=0, tiled=True).reshape(row_count, TILE, F)
    totals = sweep(
        weights_all,
        row_ids_all,
        col_ids_all,
        live_count,
        gathered,
        jnp.zeros((col_count, TILE, F), jnp.float32),
        True,
        0,
    )
    aggregate = lax.psum_scatter(
        totals.reshape(col_count * TILE, F), "col", scatter_dimension=0, tiled=True
    )
    center = jnp.mean(aggregate, axis=-1, keepdims=True)
    spread = jnp.mean(jnp.square(aggregate - center), axis=-1, keepdims=True)
    inverse = lax.rsqrt(spread + 1e-05)
    normed = (aggregate - center) * inverse
    onehot = (node_type[:, None] == jnp.arange(TYPES, dtype=jnp.int32)[None, :]).astype(jnp.float32)
    gains = jnp.dot(onehot, type_gain, precision=lax.Precision.HIGHEST)
    scaled = (normed * gains).astype(jnp.bfloat16)
    hidden = jnp.dot(scaled, w_in, preferred_element_type=jnp.float32)
    activated = jax.nn.silu(hidden).astype(jnp.bfloat16)
    branch = jnp.dot(activated, w_out, preferred_element_type=jnp.float32)
    mixed = (aggregate + branch).astype(jnp.bfloat16)
    upstream = cotangent.astype(jnp.float32)
    grad_out_w = jnp.dot(activated.T, cotangent, preferred_element_type=jnp.float32)
    grad_act = jnp.dot(cotangent, w_out.T, preferred_element_type=jnp.float32)
    sigmoid_h = jax.nn.sigmoid(hidden)
    grad_hidden = (grad_act * sigmoid_h * (1.0 + hidden * (1.0 - sigmoid_h))).astype(jnp.bfloat16)
    grad_in_w = jnp.dot(scaled.T, grad_hidden, preferred_element_type=jnp.float32)
    grad_scaled = jnp.dot(grad_hidden, w_in.T, preferred_element_type=jnp.float32)
    grad_gain = jnp.dot(onehot.T, grad_scaled * normed, precision=lax.Precision.HIGHEST)
    grad_normed = grad_scaled * gains
    grad_agg = upstream + inverse * (
        grad_normed
        - jnp.mean(grad_normed, axis=-1, keepdims=True)
        - normed * jnp.mean(grad_normed * normed, axis=-1, keepdims=True)
    )
    grad_rows = grad_agg.astype(jnp.bfloat16)
    reduced = lax.psum((grad_in_w, grad_out_w, grad_gain), ("row", "col"))
    grad_sources = lax.all_gather(grad_rows, "col", axis=0, tiled=True).reshape(col_count, TILE, F)
    back = sweep(
        weights_all,
        row_ids_all,
        col_ids_all,
        live_count,
        grad_sources,
        jnp.zeros((row_count, TILE, F), jnp.float32),
        False,
        0,
    )
    grad_x = lax.psum_scatter(
        back.reshape(row_count * TILE, F), "row", scatter_dimension=0, tiled=True
    )
    factor = float(total_nodes) ** (-0.5)
    return (mixed, grad_x, reduced[0] * factor, reduced[1] * factor, reduced[2] * factor)


def solution(mesh):
    return jax.shard_map(
        shards,
        mesh=mesh,
        in_specs=(
            P(("col", "row"), None),
            P("row", "col", None, None),
            P("row", "col"),
            P("row", "col"),
            P("row", "col"),
            P(("row", "col")),
            P(),
            P(),
            P(),
            P(("row", "col"), None),
        ),
        out_specs=(P(("row", "col"), None), P(("col", "row"), None), P(), P(), P()),
        check_vma=False,
    )
```

profile of v0, /device:TPU:1, one launch (start us, length us, event | category | flops | bytes accessed | tf_op | source)
XLA Modules:
  0.0 769.3 jit_solution(11946579066212321571)
XLA Ops:
  8.0 41.9 %all-gather.3.cloned.1.call-done = bf16[1024,512]{1,0:T(8,128)(2,1)} async-done(((bf16[128,512]{1,0:T(8,128)(2,1)}), bf16[1024,512]{1,0:T(8,128)(2,1)}) %all-gather.3.cloned.1.call-update) | async-done | bytes 1048592 | tf_op jit(solution)/shard_map/all_gather | solution.py:60
  49.9 4.3 broadcast_in_dim.90
  54.1 127.9 %while.26 = (s32[]{:T(128)}, f32[32,128,512]{2,1,0:T(8,128)}, s32[128]{0:T(128)S(1)}, s32[]{:T(128)}, bf16[128,128,128]{2,1,0:T(8,128)(2,1)}, /*index=5*/s32[128...) while((s32[]{:T(128)}, f32[32,128,512]{2,1,0:T(8,128)}, ...), condition=%wide.region_2.3_spmd, body=%wide.region_0.2_spmd.sunk | while | flops 270533856 | bytes 23597776 | solution.py:38
  55.0 1.9 gather_fusion
  56.9 3.7 convolution_select_fusion.4
  60.6 9.6 %scatter_fusion = f32[32,128,512]{2,1,0:T(8,128)} fusion(f32[32,128,512]{2,1,0:T(8,128)} %get-tuple-element.410, s32[16]{0:T(128)S(1)} %get-tuple-element.387, f32[16,128,512]{2,1,0:T(8,128)} %convolution_select_fusion.4), kind=kCustom, calls=%fused_computation.2.clone.1 | custom fusion | flops 1048576 | bytes 12582976 | tf_op jit(solution)/shard_map/while/body/eval_jaxpr/scatter-add | solution.py:36
  71.0 1.9 gather_fusion
  72.9 3.7 convolution_select_fusion.4
  76.6 9.4 %scatter_fusion = f32[32,128,512]{2,1,0:T(8,128)} fusion(f32[32,128,512]{2,1,0:T(8,128)} %get-tuple-element.410, s32[16]{0:T(128)S(1)} %get-tuple-element.387, f32[16,128,512]{2,1,0:T(8,128)} %convolution_select_fusion.4), kind=kCustom, calls=%fused_computation.2.clone.1 | custom fusion | flops 1048576 | bytes 12582976 | tf_op jit(solution)/shard_map/while/body/eval_jaxpr/scatter-add | solution.py:36
  86.8 1.9 gather_fusion
  88.7 3.7 convolution_select_fusion.4
  92.4 9.7 %scatter_fusion = f32[32,128,512]{2,1,0:T(8,128)} fusion(f32[32,128,512]{2,1,0:T(8,128)} %get-tuple-element.410, s32[16]{0:T(128)S(1)} %get-tuple-element.387, f32[16,128,512]{2,1,0:T(8,128)} %convolution_select_fusion.4), kind=kCustom, calls=%fused_computation.2.clone.1 | custom fusion | flops 1048576 | bytes 12582976 | tf_op jit(solution)/shard_map/while/body/eval_jaxpr/scatter-add | solution.py:36
  102.9 1.9 gather_fusion
  104.8 3.7 convolution_select_fusion.4
  108.5 9.7 %scatter_fusion = f32[32,128,512]{2,1,0:T(8,128)} fusion(f32[32,128,512]{2,1,0:T(8,128)} %get-tuple-element.410, s32[16]{0:T(128)S(1)} %get-tuple-element.387, f32[16,128,512]{2,1,0:T(8,128)} %convolution_select_fusion.4), kind=kCustom, calls=%fused_computation.2.clone.1 | custom fusion | flops 1048576 | bytes 12582976 | tf_op jit(solution)/shard_map/while/body/eval_jaxpr/scatter-add | solution.py:36
  119.0 1.9 gather_fusion
  120.9 3.7 convolution_select_fusion.4
  124.6 9.6 %scatter_fusion = f32[32,128,512]{2,1,0:T(8,128)} fusion(f32[32,128,512]{2,1,0:T(8,128)} %get-tuple-element.410, s32[16]{0:T(128)S(1)} %get-tuple-element.387, f32[16,128,512]{2,1,0:T(8,128)} %convolution_select_fusion.4), kind=kCustom, calls=%fused_computation.2.clone.1 | custom fusion | flops 1048576 | bytes 12582976 | tf_op jit(solution)/shard_map/while/body/eval_jaxpr/scatter-add | solution.py:36
  135.0 1.9 gather_fusion
  137.0 3.7 convolution_select_fusion.4
  140.6 9.6 %scatter_fusion = f32[32,128,512]{2,1,0:T(8,128)} fusion(f32[32,128,512]{2,1,0:T(8,128)} %get-tuple-element.410, s32[16]{0:T(128)S(1)} %get-tuple-element.387, f32[16,128,512]{2,1,0:T(8,128)} %convolution_select_fusion.4), kind=kCustom, calls=%fused_computation.2.clone.1 | custom fusion | flops 1048576 | bytes 12582976 | tf_op jit(solution)/shard_map/while/body/eval_jaxpr/scatter-add | solution.py:36
  151.0 1.9 gather_fusion
  152.9 3.7 convolution_select_fusion.4
  156.6 9.5 %scatter_fusion = f32[32,128,512]{2,1,0:T(8,128)} fusion(f32[32,128,512]{2,1,0:T(8,128)} %get-tuple-element.410, s32[16]{0:T(128)S(1)} %get-tuple-element.387, f32[16,128,512]{2,1,0:T(8,128)} %convolution_select_fusion.4), kind=kCustom, calls=%fused_computation.2.clone.1 | custom fusion | flops 1048576 | bytes 12582976 | tf_op jit(solution)/shard_map/while/body/eval_jaxpr/scatter-add | solution.py:36
  166.9 1.9 gather_fusion
  168.9 3.7 convolution_select_fusion.4
  172.5 9.5 %scatter_fusion = f32[32,128,512]{2,1,0:T(8,128)} fusion(f32[32,128,512]{2,1,0:T(8,128)} %get-tuple-element.410, s32[16]{0:T(128)S(1)} %get-tuple-element.387, f32[16,128,512]{2,1,0:T(8,128)} %convolution_select_fusion.4), kind=kCustom, calls=%fused_computation.2.clone.1 | custom fusion | flops 1048576 | bytes 12582976 | tf_op jit(solution)/shard_map/while/body/eval_jaxpr/scatter-add | solution.py:36
  182.2 155.6 %reduce-scatter.3.cloned.1.call-done = f32[128,512]{1,0:T(8,128)} async-done(((f32[4096,512]{1,0:T(8,128)}), f32[128,512]{1,0:T(8,128)}) %reduce-scatter.3.cloned.1.call-update) | async-done | bytes 262160 | tf_op jit(solution)/shard_map/reduce_scatter | solution.py:71
  341.6 1.9 fusion.5
  345.6 6.4 copy.15
  352.1 1.8 fusion.17
  353.8 1.8 fusion.14
  355.7 79.1 %all-gather.5.cloned.1.call-done = bf16[4096,512]{1,0:T(8,128)(2,1)} async-done(((bf16[128,512]{1,0:T(8,128)(2,1)}), bf16[4096,512]{1,0:T(8,128)(2,1)}) %all-gather.5.cloned.1.call-update) | async-done | bytes 4194320 | tf_op jit(solution)/shard_map/all_gather | solution.py:101
  435.1 125.2 %while.27 = (s32[]{:T(128)}, f32[8,128,512]{2,1,0:T(8,128)S(1)}, s32[128]{0:T(128)S(1)}, s32[]{:T(128)}, bf16[128,128,128]{1,2,0:T(8,128)(2,1)}, /*index=5*/s32[...) while((s32[]{:T(128)}, f32[8,128,512]{2,1,0:T(8,128)S(1)}, ...), condition=%wide.region_10.11_spmd, body=%wide.region_8.10_spmd.sunk | while | flops 270533856 | bytes 23597776 | solution.py:38
  436.0 4.2 gather_fusion.1
  440.1 4.4 convolution_select_fusion.5
  444.6 6.2 scatter_fusion.1
  451.6 4.3 gather_fusion.1
  455.9 4.4 convolution_select_fusion.5
  460.3 6.2 scatter_fusion.1
  467.3 4.2 gather_fusion.1
  471.5 4.4 convolution_select_fusion.5
  476.0 6.2 scatter_fusion.1
  483.0 4.3 gather_fusion.1
  487.3 4.4 convolution_select_fusion.5
  491.7 6.2 scatter_fusion.1
  498.8 4.2 gather_fusion.1
  503.0 4.4 convolution_select_fusion.5
  507.4 6.1 scatter_fusion.1
  514.4 4.2 gather_fusion.1
  518.6 4.4 convolution_select_fusion.5
  523.0 6.2 scatter_fusion.1
  530.0 4.2 gather_fusion.1
  534.2 4.4 convolution_select_fusion.5
  538.6 6.1 scatter_fusion.1
  545.6 4.2 gather_fusion.1
  549.8 4.4 convolution_select_fusion.5
  554.2 6.2 scatter_fusion.1
  563.0 75.5 %psum.23 = f32[8,512]{1,0:T(8,128)S(1)} all-reduce(f32[8,512]{1,0:T(8,128)S(1)} %fusion.7), channel_id=1, replica_groups=mesh['row'=8,'col'=32] {'row','col'}, use_global_device_ids=true, to_apply=%region_14.15 | all-reduce | flops 4096 | bytes 32768 | tf_op jit(solution)/shard_map/psum | solution.py:100
  639.1 2.4 fusion.6
  641.5 65.1 %all-reduce.3.cloned.1.call-done = (f32[512,1024]{1,0:T(8,128)}, f32[1024,512]{1,0:T(8,128)}) async-done(((f32[512,1024]{1,0:T(8,128)}, f32[1024,512]{1,0:T(8,128)}), (f32[512,1024]{1,0:T(8,128)}, f32[1024,512]{1,0:T(8,128)})) %all-reduce.3.cloned.1.call-update) | async-done | bytes 4194320 | tf_op jit(solution)/shard_map/psum | solution.py:100
  706.5 3.3 broadcast_multiply_fusion
  709.8 1.5 broadcast_multiply_fusion.1
  711.4 51.5 %reduce-scatter.5.cloned.1.call-done = f32[128,512]{1,0:T(8,128)} async-done(((f32[1024,512]{1,0:T(8,128)}), f32[128,512]{1,0:T(8,128)}) %reduce-scatter.5.cloned.1.call-update) | async-done | bytes 262160 | tf_op jit(solution)/shard_map/reduce_scatter | solution.py:112
  (90 shorter events, 23.2 us)
Async XLA Ops:
  7.2 334.1 %copy-start = (bf16[512,1024]{1,0:T(8,128)(2,1)S(1)}, bf16[512,1024]{1,0:T(8,128)(2,1)}, u32[]{:S(2)}) copy-start(bf16[512,1024]{1,0:T(8,128)(2,1)} %param.21) | copy-start | bytes 3145732
  7.2 42.7 %all-gather.3.cloned.1.call-start = ((), (), s32[]{:S(2)}) async-start(), calls=%async_computation.2 | async-start | bytes 1179648 | tf_op jit(solution)/shard_map/all_gather | solution.py:60
  7.9 329.8 %reduce-scatter.3.cloned.1.call-start = ((), (), s32[]{:S(2)}) async-start(), calls=%async_computation.3 | async-start | bytes 8650752 | tf_op jit(solution)/shard_map/reduce_scatter | solution.py:71
  49.8 4.3 copy-start.6
  49.9 4.3 copy-start.7
  182.1 157.9 %copy-start.8 = (f32[8,512]{1,0:T(8,128)S(1)}, f32[8,512]{1,0:T(8,128)}, u32[]{:S(2)}) copy-start(f32[8,512]{1,0:T(8,128)} %param.20) | copy-start | bytes 49156
  182.1 157.9 %copy-start.9 = (s32[128]{0:T(128)S(1)}, s32[128]{0:T(128)}, u32[]{:S(2)}) copy-start(s32[128]{0:T(128)} %param.19) | copy-start | bytes 1540
  182.1 159.5 %copy-start.5 = (bf16[128,512]{1,0:T(8,128)(2,1)S(1)}, bf16[128,512]{1,0:T(8,128)(2,1)}, u32[]{:S(2)}) copy-start(bf16[128,512]{1,0:T(8,128)(2,1)} %param.23) | copy-start | bytes 393220
  182.1 252.7 %all-gather.5.cloned.1.call-start = ((), (), s32[]{:S(2)}) async-start(), calls=%async_computation.4 | async-start | bytes 4325376 | tf_op jit(solution)/shard_map/all_gather | solution.py:101
  341.6 12.3 %copy-start.4 = (f32[128,1024]{1,0:T(8,128)}, f32[128,1024]{1,0:T(8,128)S(1)}, u32[]{:S(2)}) copy-start(f32[128,1024]{1,0:T(8,128)S(1)} %fusion.16) | copy-start | bytes 1572868
  341.6 1.9 copy-start.2
  345.6 360.9 %all-reduce.3.cloned.1.call-start = ((), (), s32[]{:S(2)}) async-start(), calls=%async_computation.6 | async-start | bytes 8388608 | tf_op jit(solution)/shard_map/psum | solution.py:100
  355.7 407.2 %reduce-scatter.5.cloned.1.call-start = ((), (), s32[]{:S(2)}) async-start(), calls=%async_computation.5 | async-start | bytes 2359296 | tf_op jit(solution)/shard_map/reduce_scatter | solution.py:112
  560.3 1.3 copy-start.1
  706.5 3.3 copy-start.3
Sparse Core Ops, SparseCore 0:
  9.8 40.0 all-gather.2
  182.2 155.4 reduce-scatter.2
  345.7 89.1 all-gather.4
  440.9 265.5 all-reduce.2
  709.5 53.2 reduce-scatter.4
where the time goes:
time: 773 us; the launch traced here: 769 us
  waiting for transfers between devices  394 us (51%)
  other arithmetic  147 us (19%)
  matrix products  76.7 us (10%)
  blocking collectives  75.5 us (10%)
  local copies, waits for them, and re-layouts  61.3 us (8%)
  between operations  13.9 us (2%)
    reduce_scatter x1, waiting for transfers between devices, shards(): lax.psum_scatter(totals.reshape(col_count * TILE, F), 'col', scatter_dime...  156 us
    scatter-add x16, other arithmetic, advance(): return totals.at[placed].add(product)  126 us
    all_gather x1, waiting for transfers between devices, shards(): lax.all_gather(grad_rows, 'col', axis=0, tiled=True)  79.1 us
    psum x1, blocking collectives, shards(): reduced = lax.psum((grad_in_w, grad_out_w, grad_gain), ('row', 'col'))  75.5 us
    psum x1, waiting for transfers between devices, shards(): reduced = lax.psum((grad_in_w, grad_out_w, grad_gain), ('row', 'col'))  65.1 us
    reduce_scatter x1, waiting for transfers between devices, shards(): lax.psum_scatter(back.reshape(row_count * TILE, F), 'row', scatter_dimens...  51.5 us
    all_gather x1, waiting for transfers between devices, shards(): lax.all_gather(features, 'row', axis=0, tiled=True)  41.9 us
    dot_general x8, matrix products, advance(): jnp.einsum('sab,saf->sbf', weights_now, pieces, preferred_element_type=jn...  35.3 us
  transfers between devices with their start and end apart: 5, of which 5 were waited for; matrix products, arithmetic and copies ran while one was open for 19% of the time, Pallas kernels for 0%

commit v1 on v0

v1 whole, which is shorter than its diff:
```python
import functools

import jax
import jax.numpy as jnp
from jax import lax
from jax.experimental import pallas as pl
from jax.experimental.pallas import tpu as pltpu
from jax.sharding import PartitionSpec as P

F = 512
TYPES = 8
TILE = 128
GROUP = 16
UNROLL = 4
HALF = TILE // 2
MESH = pl.DeviceIdType.MESH
BF = jnp.bfloat16
F32 = jnp.float32


def sweep_body(forward, spare, count, rows, cols, weights, sources, out, acc):
    step = pl.program_id(0)

    @pl.when(step == 0)
    def _():
        acc[...] = jnp.zeros_like(acc)

    first = step * GROUP
    live = count[0]
    rounds = jnp.clip((live - first + UNROLL - 1) // UNROLL, 0, GROUP // UNROLL)

    def advance(block, carry):
        products = []
        places = []
        for u in range(UNROLL):
            inner = block * UNROLL + u
            slot = first + inner
            source, place = (cols[slot], rows[slot]) if forward else (rows[slot], cols[slot])
            places.append(jnp.where(slot < live, place, spare))
            contract = ((1,), (0,)) if forward else ((0,), (0,))
            products.append(
                lax.dot_general(
                    weights[inner],
                    sources[source],
                    (contract, ((), ())),
                    preferred_element_type=jnp.float32,
                )
            )
        for place, product in zip(places, products):
            acc[place] += product
        return carry

    lax.fori_loop(0, rounds, advance, 0)

    @pl.when(step == pl.num_programs(0) - 1)
    def _():
        for tile in range(spare):
            out[tile] = acc[tile].astype(out.dtype)


def sweep(weights_all, row_ids, col_ids, live_count, sources, spare, forward, dtype):
    slots = weights_all.shape[0]
    last = lambda count: (count[0] - 1) // GROUP
    return pl.pallas_call(
        functools.partial(sweep_body, forward, spare),
        grid_spec=pltpu.PrefetchScalarGridSpec(
            num_scalar_prefetch=3,
            grid=(slots // GROUP,),
            in_specs=[
                pl.BlockSpec(
                    (GROUP, TILE, TILE), lambda i, n, r, c: (jnp.minimum(i, last(n)), 0, 0)
                ),
                pl.BlockSpec(sources.shape, lambda i, n, r, c: (0, 0, 0)),
            ],
            out_specs=pl.BlockSpec((spare, TILE, F), lambda i, n, r, c: (0, 0, 0)),
            scratch_shapes=[pltpu.VMEM((spare + 1, TILE, F), jnp.float32)],
        ),
        out_shape=jax.ShapeDtypeStruct((spare, TILE, F), dtype),
        name="sweep_forward" if forward else "sweep_backward",
    )(live_count, row_ids, col_ids, weights_all, sources)


class Place:
    def __init__(self):
        row = lax.axis_index("row")
        col = lax.axis_index("col")
        self.row, self.col = row, col
        self.x, self.low = row // 2, row % 2
        self.high, self.z, self.core = col // 16, (col // 2) % 8, col % 2
        self.y = self.high * 2 + self.low

    def at(self, x=None, y=None, z=None, core=None):
        x = self.x if x is None else x
        y = self.y if y is None else y
        z = self.z if z is None else z
        core = self.core if core is None else core
        return (x * 2 + y % 2, (y // 2) * 16 + z * 2 + core)

    def along(self, axis, offset):
        size = {"x": 4, "y": 4, "z": 8}[axis]
        return self.at(**{axis: (getattr(self, axis) + offset + size) % size})


class Wire:
    def __init__(self, send, recv):
        self.send, self.recv, self.copies = send, recv, []

    def push(self, source, target, device):
        index = len(self.copies)
        copy = pltpu.make_async_remote_copy(
            src_ref=source,
            dst_ref=target,
            send_sem=self.send.at[index],
            recv_sem=self.recv.at[index],
            device_id=device,
            device_id_type=MESH,
        )
        copy.start()
        self.copies.append([copy, False])
        return index

    def arrived(self, index):
        if not self.copies[index][1]:
            self.copies[index][0].wait_recv()
            self.copies[index][1] = True

    def finish(self):
        for index, (copy, _) in enumerate(self.copies):
            self.arrived(index)
            copy.wait_send()


def enter(devices):
    barrier = pltpu.get_barrier_semaphore()
    for device in devices:
        pl.semaphore_signal(barrier, inc=1, device_id=device, device_id_type=MESH)
    pl.semaphore_wait(barrier, len(devices))


def halves(size):
    return (pl.ds(0, size // 2), pl.ds(size // 2, size // 2))


def remote_call(body, name, ident, outs, in_spaces, scratch, copies, args):
    return pl.pallas_call(
        body,
        out_shape=outs,
        in_specs=[pl.BlockSpec(memory_space=space) for space in in_spaces],
        out_specs=[pl.BlockSpec(memory_space=pltpu.VMEM)] * len(outs),
        scratch_shapes=list(scratch)
        + [pltpu.SemaphoreType.DMA((copies,)), pltpu.SemaphoreType.DMA((copies,))],
        compiler_params=pltpu.CompilerParams(
            collective_id=ident, has_side_effects=True, vmem_limit_bytes=60 * 2**20
        ),
        name=name,
    )(*args)


def gather_body(features, out, send, recv):
    me, wire = Place(), Wire(send, recv)
    right, left = me.along("x", 1), me.along("x", -1)
    mate = me.at(y=me.high * 2 + 1 - me.low)
    enter([mate, right, left])
    row = me.row
    first = wire.push(features, out.at[row], mate)
    own = [wire.push(features, out.at[row], device) for device in (right, left)]
    out[row] = features[...]
    wire.arrived(first)
    row_mate = me.x * 2 + 1 - me.low
    other = [wire.push(out.at[row_mate], out.at[row_mate], device) for device in (right, left)]
    for pair, low in ((own, me.low), (other, 1 - me.low)):
        for side, rows in enumerate(halves(TILE)):
            wire.arrived(pair[side])
            held = ((me.x + (3 if side == 0 else 1)) % 4) * 2 + low
            wire.push(out.at[held, rows], out.at[held, rows], (right, left)[side])
    wire.finish()


def contract(a, b, left, right):
    return lax.dot_general(a, b, (((left,), (right,)), ((), ())), preferred_element_type=F32)


OFFSETS = (4, 3, 5, 2, 6, 1, 7, 0)


def dense_body(
    totals, cot, kinds, table, w_in, w_out,
    mixed, gathered, w_part, g_part,
    own, sib, z_out, z_in, y_out, y_in, mine, grad_act, gains,
    scaled2, act_half, act2, hid_half, hid2, cot2,
    weights, x_out, x_in, summed, v_out, v_in, g_out, g_in,
    local, send, recv,
):
    me, wire = Place(), Wire(send, recv)
    twin = me.at(core=1 - me.core)
    across = me.along("y", 2)
    z_side = (me.along("z", 1), me.along("z", -1))
    x_side = (me.along("x", 1), me.along("x", -1))
    y_side = (me.along("y", 1), me.along("y", -1))
    enter([twin, across, *z_side, *x_side, *y_side])

    loads, parts = {}, {}
    for order, offset in enumerate(OFFSETS):
        for side in range(2):
            slot = order * 2 + side
            tile = ((me.high + 1 + side) % 2) * 16 + ((me.z + offset) % 8) * 2
            load = pltpu.make_async_copy(totals.at[tile + me.core], own.at[slot], local.at[slot])
            load.start()
            loads[slot] = load
            parts[slot] = wire.push(totals.at[tile + 1 - me.core], sib.at[slot], twin)
    cot_sent = wire.push(cot, cot2.at[pl.ds(TILE, TILE)], twin)
    cot2[0:TILE] = cot[...]
    grad_act[...] = contract(cot[...], w_out[...], 1, 1)
    kind = kinds[...]
    chosen = jnp.zeros((TILE, F), F32)
    for t in range(TYPES):
        chosen = jnp.where(kind == t, table[t : t + 1], chosen)
    gains[...] = chosen

    def base(offset, side):
        slot = OFFSETS.index(offset) * 2 + side
        if slot in loads:
            loads.pop(slot).wait()
            wire.arrived(parts[slot])
        return slot

    sent = {}
    for hop in (4, 3, 2, 1):
        for side in range(2):
            for turn in range(2):
                offset = hop if turn == 0 else 8 - hop
                slot = base(offset, side)
                stage = z_out.at[turn, side, hop - 1]
                for part, rows in enumerate(halves(TILE)):
                    if hop == 4 and part != turn:
                        continue
                    value = own[slot, rows] + sib[slot, rows]
                    if hop < 3 or (hop == 3 and part == turn):
                        wire.arrived(sent[turn, side, hop + 1])
                        value = value + z_in[turn, side, hop, rows].astype(F32)
                    stage[rows] = value.astype(BF)
                moved = halves(TILE)[turn] if hop == 4 else pl.ds(0, TILE)
                sent[turn, side, hop] = wire.push(
                    z_out.at[turn, side, hop - 1, moved],
                    z_in.at[turn, side, hop - 1, moved],
                    z_side[turn],
                )
    ends = []
    for side in range(2):
        slot = base(0, side)
        value = own[slot] + sib[slot]
        for turn in range(2):
            wire.arrived(sent[turn, side, 1])
            value = value + z_in[turn, side, 0].astype(F32)
        if side == 0:
            y_out[...] = value.astype(BF)
            crossed = wire.push(y_out, y_in, across)
        else:
            ends.append(value)
    wire.arrived(crossed)
    aggregate = ends[0] + y_in[...].astype(F32)

    center = jnp.mean(aggregate, axis=-1, keepdims=True)
    spread = jnp.mean(jnp.square(aggregate - center), axis=-1, keepdims=True)
    inverse = lax.rsqrt(spread + 1e-05)
    normed = (aggregate - center) * inverse
    scaled = (normed * gains[...]).astype(BF)
    scaled2[0:TILE] = scaled
    scaled_sent = wire.push(scaled2.at[pl.ds(0, TILE)], scaled2.at[pl.ds(TILE, TILE)], twin)
    hidden = contract(scaled, w_in[...], 1, 0)
    sigmoid = jax.nn.sigmoid(hidden)
    activated = (hidden * sigmoid).astype(BF)
    grad_hidden = (grad_act[...] * sigmoid * (1.0 + hidden * (1.0 - sigmoid))).astype(BF)
    grad_scaled = contract(grad_hidden, w_in[...], 1, 1)
    grad_normed = grad_scaled * gains[...]
    grad_rows = (
        cot[...].astype(F32)
        + inverse
        * (
            grad_normed
            - jnp.mean(grad_normed, axis=-1, keepdims=True)
            - normed * jnp.mean(grad_normed * normed, axis=-1, keepdims=True)
        )
    ).astype(BF)
    mine[...] = grad_rows
    col = me.col
    crossed = wire.push(mine, gathered.at[col], across)
    own_sent = [wire.push(mine, gathered.at[col], device) for device in z_side]
    wire.push(mine, gathered.at[col], twin)
    gathered[col] = grad_rows
    for half in range(2):
        act_half[half] = activated[:, half * F : (half + 1) * F]
        hid_half[half] = grad_hidden[:, half * F : (half + 1) * F]
    late = pl.ds(TILE, TILE)
    act_sent = wire.push(act_half.at[1 - me.core], act2.at[late], twin)
    hid_sent = wire.push(hid_half.at[1 - me.core], hid2.at[late], twin)
    act2[0:TILE] = act_half[me.core]
    hid2[0:TILE] = hid_half[me.core]
    product = grad_scaled * normed
    for t in range(TYPES):
        g_out[0, t : t + 1] = jnp.sum(jnp.where(kind == t, product, 0.0), axis=0, keepdims=True)
    gain_sent = wire.push(g_out.at[0], g_in.at[0], twin)

    def index_of(family, offset):
        high = me.high if family == 0 else 1 - me.high
        return high * 16 + ((me.z + offset + 8) % 8) * 2 + me.core

    wire.arrived(crossed)
    place = index_of(1, 0)
    other_sent = [
        wire.push(gathered.at[place], gathered.at[place], device) for device in z_side
    ]
    wire.push(gathered.at[place], gathered.at[place], twin)
    mixed[...] = (aggregate + contract(activated, w_out[...], 1, 0)).astype(BF)
    flows = [own_sent, other_sent]

    def forward(hop):
        for family in range(2):
            for turn in range(2):
                wire.arrived(flows[family][turn])
                place = index_of(family, (1 - hop) if turn == 0 else (hop - 1))
                moved = halves(TILE)[turn] if hop == 4 else pl.ds(0, TILE)
                flows[family][turn] = wire.push(
                    gathered.at[place, moved], gathered.at[place, moved], z_side[turn]
                )
                wire.push(gathered.at[place], gathered.at[place], twin)

    forward(2)

    for arrival in (cot_sent, scaled_sent, act_sent, hid_sent, gain_sent):
        wire.arrived(arrival)
    for part in range(4):
        columns = slice((part % 2) * 256, (part % 2) * 256 + 256)
        if part < 2:
            weights[part] = contract(act2[:, columns], cot2[...], 0, 0)
        else:
            weights[part] = contract(scaled2[:, columns], hid2[...], 0, 0)

    def gain_step(phase, device):
        g_out[phase] = g_out[phase - 1] + g_in[phase - 1]
        return wire.push(g_out.at[phase], g_in.at[phase], device)

    gain_sent = gain_step(1, me.at(x=me.x + 1 - 2 * (me.x % 2)))
    ring = []
    quarter = halves(256)
    far = (me.x + 2) % 4
    for turn in range(2):
        x_out[turn, 1, quarter[turn]] = weights[far, quarter[turn]].astype(BF)
        ring.append(
            wire.push(
                x_out.at[turn, 1, quarter[turn]], x_in.at[turn, 1, quarter[turn]], x_side[turn]
            )
        )
    forward(3)
    wire.arrived(gain_sent)
    gain_sent = gain_step(2, me.at(x=3 - me.x))
    for turn in range(2):
        wire.arrived(ring[turn])
        near = (me.x + (1 if turn == 0 else 3)) % 4
        x_out[turn, 0, quarter[1 - turn]] = weights[near, quarter[1 - turn]].astype(BF)
        x_out[turn, 0, quarter[turn]] = (
            weights[near, quarter[turn]] + x_in[turn, 1, quarter[turn]].astype(F32)
        ).astype(BF)
        ring[turn] = wire.push(x_out.at[turn, 0], x_in.at[turn, 0], x_side[turn])
    forward(4)
    wire.arrived(gain_sent)
    gain_sent = gain_step(3, me.at(y=me.y + 1 - 2 * (me.y % 2)))
    for turn in range(2):
        wire.arrived(ring[turn])
    for part in range(4):
        rows = pl.ds(part * 64, 64)
        summed[part] = (
            weights[me.x, rows] + x_in[0, 0, rows].astype(F32) + x_in[1, 0, rows].astype(F32)
        )
    eighth = halves(64)
    far = (me.y + 2) % 4
    for turn in range(2):
        v_out[turn, 1, eighth[turn]] = summed[far, eighth[turn]]
        ring[turn] = wire.push(
            v_out.at[turn, 1, eighth[turn]], v_in.at[turn, 1, eighth[turn]], y_side[turn]
        )
    wire.arrived(gain_sent)
    gain_sent = gain_step(4, me.at(y=3 - me.y))
    for turn in range(2):
        wire.arrived(ring[turn])
        near = (me.y + (1 if turn == 0 else 3)) % 4
        v_out[turn, 0, eighth[1 - turn]] = summed[near, eighth[1 - turn]]
        v_out[turn, 0, eighth[turn]] = summed[near, eighth[turn]] + v_in[turn, 1, eighth[turn]]
        ring[turn] = wire.push(v_out.at[turn, 0], v_in.at[turn, 0], y_side[turn])
    for family in range(2):
        for turn in range(2):
            wire.arrived(flows[family][turn])
        place = index_of(family, 4)
        wire.push(gathered.at[place], gathered.at[place], twin)
    for turn in range(2):
        wire.arrived(ring[turn])
    for part in range(8):
        rows = pl.ds(part * 8, 8)
        w_part[part] = summed[me.y, rows] + v_in[0, 0, rows] + v_in[1, 0, rows]
    wire.arrived(gain_sent)
    g_part[...] = g_out[4] + g_in[4]
    wire.finish()


def finish_body(
    factor, back, w_part, g_part, grad_x, w_all, gain,
    z_in, x_out, x_in, y_out, y_in, piece, g_out, g_in, send, recv,
):
    me, wire = Place(), Wire(send, recv)
    twin = me.at(core=1 - me.core)
    z_all = [me.along("z", step) for step in range(1, 8)]
    x_side = (me.along("x", 1), me.along("x", -1))
    y_side = (me.along("y", 1), me.along("y", -1))
    mate = me.at(y=me.high * 2 + 1 - me.low)
    enter([twin, *z_all, *x_side, *y_side])

    scattered = [
        wire.push(w_part.at[(me.z + step) % 8], z_in.at[step - 1], z_all[step - 1])
        for step in range(1, 8)
    ]
    gain_sent = wire.push(g_part, g_in.at[0], me.at(z=me.z + 1 - 2 * (me.z % 2)))
    ring = {}
    for side in range(2):
        low = (me.low + 1 + side) % 2
        far = ((me.x + 2) % 4) * 2 + low
        for turn, rows in enumerate(halves(TILE)):
            x_out[turn, side, 1, rows] = back[far, rows].astype(BF)
            ring[turn, side] = wire.push(
                x_out.at[turn, side, 1, rows], x_in.at[turn, side, 1, rows], x_side[turn]
            )
    total = w_part[me.z]
    for step in range(7):
        wire.arrived(scattered[step])
        total = total + z_in[step]
    total = (total * factor).astype(BF)
    piece[...] = total
    w_all[me.core, me.x, me.y, me.z] = total
    spot = w_all.at[me.core, me.x, me.y, me.z]
    spread = [wire.push(piece, spot, device) for device in z_all]
    wire.arrived(gain_sent)
    base = (me.z // 4) * 4
    g_out[0] = g_part[...] + g_in[0]
    gain_sent = wire.push(g_out.at[0], g_in.at[1], me.at(z=base + 3 - me.z % 4))
    for side in range(2):
        low = (me.low + 1 + side) % 2
        for turn, rows in enumerate(halves(TILE)):
            wire.arrived(ring[turn, side])
            near = ((me.x + (1 if turn == 0 else 3)) % 4) * 2 + low
            rest = halves(TILE)[1 - turn]
            x_out[turn, side, 0, rest] = back[near, rest].astype(BF)
            x_out[turn, side, 0, rows] = (
                back[near, rows] + x_in[turn, side, 1, rows].astype(F32)
            ).astype(BF)
            ring[turn, side] = wire.push(
                x_out.at[turn, side, 0], x_in.at[turn, side, 0], x_side[turn]
            )
    wire.arrived(gain_sent)
    g_out[1] = g_out[0] + g_in[1]
    gain_sent = wire.push(g_out.at[1], g_in.at[2], me.at(z=(me.z + 4) % 8))
    for index in spread:
        wire.arrived(index)
    core = me.core
    block = w_all.at[core, me.x, me.y]
    column = [wire.push(block, block, device) for device in y_side]
    ends = []
    for side in range(2):
        low = (me.low + 1 + side) % 2
        value = back[me.x * 2 + low]
        for turn in range(2):
            wire.arrived(ring[turn, side])
            value = value + x_in[turn, side, 0].astype(F32)
        if side == 0:
            y_out[...] = value.astype(BF)
            crossed = wire.push(y_out, y_in, mate)
        else:
            ends.append(value)
    for turn, rows in enumerate((pl.ds(0, 4), pl.ds(4, 4))):
        wire.arrived(column[turn])
        held = (me.y + (3 if turn == 0 else 1)) % 4
        view = w_all.at[core, me.x, held, rows]
        column[turn] = wire.push(view, view, y_side[turn])
    for turn in range(2):
        wire.arrived(column[turn])
    block = w_all.at[core, me.x]
    plane = [wire.push(block, block, device) for device in x_side]
    wire.push(block, block, twin)
    wire.arrived(crossed)
    grad_x[...] = ends[0] + y_in[...].astype(F32)
    wire.arrived(gain_sent)
    gain[...] = (g_out[1] + g_in[2]) * factor
    for turn, rows in enumerate((pl.ds(0, 2), pl.ds(2, 2))):
        wire.arrived(plane[turn])
        held = (me.x + (3 if turn == 0 else 1)) % 4
        view = w_all.at[core, held, rows]
        plane[turn] = wire.push(view, view, x_side[turn])
        block = w_all.at[core, held]
        wire.push(block, block, twin)
    for turn in range(2):
        wire.arrived(plane[turn])
    block = w_all.at[core, (me.x + 2) % 4]
    wire.push(block, block, twin)
    wire.finish()


def shards(
    features,
    tile_vals,
    tile_row,
    tile_col,
    tile_count,
    node_type,
    type_gain,
    w_in,
    w_out,
    cotangent,
):
    row_count = lax.axis_size("row")
    col_count = lax.axis_size("col")
    hid = w_in.shape[1]
    total_nodes = TILE * row_count * col_count
    factor = float(total_nodes) ** (-0.5)
    weights_all, row_ids, col_ids = tile_vals[0], tile_row[0], tile_col[0]
    live_count = tile_count[0]
    shape = jax.ShapeDtypeStruct
    vmem = pltpu.VMEM
    (gathered,) = remote_call(
        gather_body, "gather_features", 1,
        [shape((row_count, TILE, F), BF)], [vmem], [], 9, (features,),
    )
    totals = sweep(weights_all, row_ids, col_ids, live_count, gathered, col_count, True, F32)
    mixed, grad_sources, w_part, g_part = remote_call(
        dense_body, "dense", 2,
        [
            shape((TILE, F), BF),
            shape((col_count, TILE, F), BF),
            shape((8, 8, F), F32),
            shape((TYPES, F), F32),
        ],
        [pl.ANY] + [vmem] * 5,
        [
            vmem((16, TILE, F), F32), vmem((16, TILE, F), F32),
            vmem((2, 2, 4, TILE, F), BF), vmem((2, 2, 4, TILE, F), BF),
            vmem((TILE, F), BF), vmem((TILE, F), BF), vmem((TILE, F), BF),
            vmem((TILE, hid), F32), vmem((TILE, F), F32),
            vmem((2 * TILE, F), BF), vmem((2, TILE, F), BF), vmem((2 * TILE, F), BF),
            vmem((2, TILE, F), BF), vmem((2 * TILE, F), BF), vmem((2 * TILE, F), BF),
            vmem((4, 256, F), F32), vmem((2, 2, 256, F), BF), vmem((2, 2, 256, F), BF),
            vmem((4, 64, F), F32), vmem((2, 2, 64, F), F32), vmem((2, 2, 64, F), F32),
            vmem((5, TYPES, F), F32), vmem((5, TYPES, F), F32),
            pltpu.SemaphoreType.DMA((16,)),
        ],
        96,
        (totals, cotangent, node_type[:, None], type_gain, w_in, w_out),
    )
    back = sweep(weights_all, row_ids, col_ids, live_count, grad_sources, row_count, False, F32)
    grad_x, w_all, gain = remote_call(
        functools.partial(finish_body, factor), "finish", 3,
        [
            shape((TILE, F), F32),
            shape((2, 4, 4, 8, 8, F), BF),
            shape((TYPES, F), F32),
        ],
        [vmem] * 3,
        [
            vmem((7, 8, F), F32),
            vmem((2, 2, 2, TILE, F), BF), vmem((2, 2, 2, TILE, F), BF),
            vmem((TILE, F), BF), vmem((TILE, F), BF), vmem((8, F), BF),
            vmem((2, TYPES, F), F32), vmem((3, TYPES, F), F32),
        ],
        48,
        (back, w_part, g_part),
    )
    w_all = w_all.reshape(2, 2, 512, F).astype(F32)
    grad_w_out = w_all[:, 0].reshape(hid, F)
    grad_w_in = jnp.concatenate([w_all[0, 1], w_all[1, 1]], axis=1)
    return (mixed, grad_x, grad_w_in, grad_w_out, gain)


def solution(mesh):
    return jax.shard_map(
        shards,
        mesh=mesh,
        in_specs=(
            P(("col", "row"), None),
            P("row", "col", None, None),
            P("row", "col"),
            P("row", "col"),
            P("row", "col"),
            P(("row", "col")),
            P(),
            P(),
            P(),
            P(("row", "col"), None),
        ),
        out_specs=(P(("row", "col"), None), P(("col", "row"), None), P(), P(), P()),
        check_vma=False,
    )
```

time: 773 us -> 166 us (0.21)
  waiting for transfers between devices: 394 us -> 0 us
  Pallas kernels: 0 us -> 156 us
  other arithmetic: 147 us -> 2.03 us
  matrix products: 76.7 us -> 0 us
  blocking collectives: 75.5 us -> 0 us
  local copies, waits for them, and re-layouts: 61.3 us -> 6.53 us
  between operations: 13.9 us -> 1.35 us
    reduce_scatter x2 -> x0, waiting for transfers between devices: 207 us -> none  [the longest x1 156 us: shards(): lax.psum_scatter(totals.reshape(col_count * TILE, F), 'col', scatter_dime...]
    pallas_call x0 -> x5, Pallas kernels: none -> 156 us  [the longest x3 143 us: remote_call(): pl.pallas_call(body, out_shape=outs, in_specs=[pl.BlockSpec(memory_space=...]
    scatter-add x16 -> x0, other arithmetic: 126 us -> none  [advance(): return totals.at[placed].add(product)]
    all_gather x2 -> x0, waiting for transfers between devices: 121 us -> none  [the longest x1 79.1 us: shards(): lax.all_gather(grad_rows, 'col', axis=0, tiled=True)]
    dot_general x24 -> x0, matrix products: 76.7 us -> none  [the longest x8 35.3 us: advance(): jnp.einsum('sab,saf->sbf', weights_now, pieces, preferred_element_type=jn...]
    psum x1 -> x0, blocking collectives: 75.5 us -> none  [shards(): reduced = lax.psum((grad_in_w, grad_out_w, grad_gain), ('row', 'col'))]
    psum x1 -> x0, waiting for transfers between devices: 65.1 us -> none  [shards(): reduced = lax.psum((grad_in_w, grad_out_w, grad_gain), ('row', 'col'))]
    gather x16 -> x0, local copies, waits for them, and re-layouts: 49 us -> none  [the longest x8 33.8 us: advance(): pieces = sources[row_ids]]
  transfers between devices with their start and end apart: 5 -> 0, of which waited for: 5 -> 0; matrix products, arithmetic and copies ran while one was open for 19% -> 0% of each run, Pallas kernels for 0% -> 0%
where the time goes in v1:
time: 166 us
  Pallas kernels  156 us (94%)
  local copies, waits for them, and re-layouts  6.53 us (4%)
  other arithmetic  2.03 us (1%)
    pallas_call x3, Pallas kernels, remote_call(): pl.pallas_call(body, out_shape=outs, in_specs=[pl.BlockSpec(memory_space=...  143 us
    pallas_call x2, Pallas kernels, sweep(): pl.pallas_call(functools.partial(sweep_body, forward, spare), grid_spec=p...  13.1 us

profile of v1, /device:TPU:1, one launch (start us, length us, event | category | flops | bytes accessed | tf_op | source)
XLA Modules:
  0.0 165.8 jit_solution(8822267451337341214)
XLA Ops:
  1.3 1.4 copy.15.kinds
  2.7 16.1 %gather_features.1.sources = bf16[8,128,512]{2,1,0:T(8,128)(2,1)} custom-call(bf16[128,512]{1,0:T(8,128)(2,1)} %features.1), custom_call_target="tpu_custom_call" | custom-call | tf_op jit(solution)/shard_map/gather_features/pallas_call | solution.py:145
  18.8 7.4 %sweep_forward.1.totals = f32[32,128,512]{2,1,0:T(8,128)} custom-call(s32[1]{0:T(128)} %bitcast.12.count, s32[128]{0:T(128)} %bitcast.19, s32[128]{0:T(128)} %bitcast.21, bf16[128,128,128]{2,1,0:T(8,128)(2,1)} %bitcast.14, bf16[8,128,512]{2,1,0:T(8,128)(2,1)} %gather_features.1.sources), custom_call_target="tpu_custom_call" | custom-call | tf_op jit(solution)/shard_map/sweep_forward/pallas_call | solution.py:64
  26.1 77.8 %dense.1 = (bf16[128,512]{1,0:T(8,128)(2,1)}, bf16[32,128,512]{2,1,0:T(8,128)(2,1)}, f32[8,8,512]{2,1,0:T(8,128)}, f32[8,512]{1,0:T(8,128)}) custom-call(f32[32,128,512]{2,1,0:T(8,128)} %sweep_forward.1.totals, bf16[128,512]{1,0:T(8,128)(2,1)} %cot.1, s32[128,1]{1,0:T(8,128)} %copy.15.kinds, f32[8,512]{1,0:T(8,128)} %table.1, bf16[512,1024]{1,0:T(8,128)(2,1)} %w_in.1, ...), custom_call_target="tpu_custom_call" | custom-call | tf_op jit(solution)/shard_map/dense/pallas_call | solution.py:145
  104.0 5.7 %sweep_backward.1.back = f32[8,128,512]{2,1,0:T(8,128)} custom-call(s32[1]{0:T(128)} %bitcast.13.count, s32[128]{0:T(128)} %bitcast.20, s32[128]{0:T(128)} %bitcast.22, bf16[128,128,128]{2,1,0:T(8,128)(2,1)} %bitcast.15, bf16[32,128,512]{2,1,0:T(8,128)(2,1)} %get-tuple-element.13.sources), custom_call_target="tpu_custom_call" | custom-call | tf_op jit(solution)/shard_map/sweep_backward/pallas_call | solution.py:64
  109.7 48.9 %finish.1 = (f32[128,512]{1,0:T(8,128)}, bf16[2,4,4,8,8,512]{5,4,3,2,1,0:T(8,128)(2,1)}, f32[8,512]{1,0:T(8,128)}) custom-call(f32[8,128,512]{2,1,0:T(8,128)} %sweep_backward.1.back, f32[8,8,512]{2,1,0:T(8,128)} %get-tuple-element.14.w_part, f32[8,512]{1,0:T(8,128)} %get-tuple-element.15.g_part), custom_call_target="tpu_custom_call" | custom-call | tf_op jit(solution)/shard_map/finish/pallas_call | solution.py:145
  158.6 0.0 copy-start
  158.6 3.0 %slice.14 = f32[2,1,512,512]{3,2,1,0:T(8,128)} slice(bf16[2,2,512,512]{3,2,1,0:T(8,128)(2,1)} %bitcast.16), slice={[0:2], [0:1], [0:512], [0:512]} | slice | bytes 4194304 | tf_op jit(solution)/shard_map/slice | solution.py:574
  161.6 0.0 copy-done
  161.6 0.6 convert.1
  162.2 0.2 slice_bitcast_fusion.1
  162.4 0.0 copy-start.2
  162.4 0.0 copy-start.1
  162.4 0.0 copy-start.3
  162.4 1.5 pad_maximum_fusion
  163.9 0.0 copy-done.2
  163.9 0.7 copy.20
  164.5 0.0 copy-done.1
  164.5 0.7 copy.21
  165.2 0.0 copy-done.3
  165.2 0.6 copy.22
Async XLA Ops:
  158.6 3.0 %copy-start = (bf16[2,4,4,8,8,512]{5,4,3,2,1,0:T(8,128)(2,1)S(1)}, bf16[2,4,4,8,8,512]{5,4,3,2,1,0:T(8,128)(2,1)}, u32[]{:S(2)}) copy-start(bf16[2,4,4,8,8,512]{5,4,3,2,1,0:T(8,128)(2,1)} %get-tuple-element.17) | copy-start | bytes 6291460
  162.4 1.5 copy-start.2
  162.4 2.1 %copy-start.1 = (f32[128,512]{1,0:T(8,128)S(1)}, f32[128,512]{1,0:T(8,128)}, u32[]{:S(2)}) copy-start(f32[128,512]{1,0:T(8,128)} %get-tuple-element.27) | copy-start | bytes 786436
  162.4 2.8 %copy-start.3 = (f32[8,512]{1,0:T(8,128)S(1)}, f32[8,512]{1,0:T(8,128)}, u32[]{:S(2)}) copy-start(f32[8,512]{1,0:T(8,128)} %get-tuple-element.30) | copy-start | bytes 49156

commit v2 on v0

v2 whole, which is shorter than its diff:
```python
import functools

import jax
import jax.numpy as jnp
from jax import lax
from jax.experimental import pallas as pl
from jax.experimental.pallas import tpu as pltpu
from jax.sharding import PartitionSpec as P

F = 512
TYPES = 8
TILE = 128
GROUP = 16
UNROLL = 4
PHASES = 8
MESH = pl.DeviceIdType.MESH
BF = jnp.bfloat16
F32 = jnp.float32
OFFSETS = (4, 3, 5, 2, 6, 1, 7, 0)


def build_body(count, rows, cols, weights, out, acc):
    step = pl.program_id(0)

    @pl.when(step == 0)
    def _():
        acc[...] = jnp.zeros_like(acc)

    first = step * GROUP
    rounds = jnp.clip((count[0] - first + UNROLL - 1) // UNROLL, 0, GROUP // UNROLL)

    @pl.when(step < PHASES)
    def _():
        def advance(block, carry):
            for u in range(UNROLL):
                inner = block * UNROLL + u
                slot = first + inner
                place = jnp.where(slot < count[0], rows[slot], acc.shape[0] - 1)
                lanes = pl.ds(pl.multiple_of(cols[slot] * TILE, TILE), TILE)
                acc[place, :, lanes] += weights[inner].astype(F32)
            return carry

        lax.fori_loop(0, rounds, advance, 0)

    @pl.when(step >= PHASES)
    def _():
        for part in range(out.shape[0]):
            out[part] = acc[(step - PHASES) * out.shape[0] + part].astype(BF)


def build(weights_all, row_ids, col_ids, live_count, tall, wide):
    last = lambda count: (count[0] - 1) // GROUP
    return pl.pallas_call(
        build_body,
        grid_spec=pltpu.PrefetchScalarGridSpec(
            num_scalar_prefetch=3,
            grid=(2 * PHASES,),
            in_specs=[
                pl.BlockSpec(
                    (GROUP, TILE, TILE), lambda i, n, r, c: (jnp.minimum(i, last(n)), 0, 0)
                ),
            ],
            out_specs=pl.BlockSpec(
                (tall // PHASES, TILE, wide), lambda i, n, r, c: (jnp.maximum(i - PHASES, 0), 0, 0)
            ),
            scratch_shapes=[pltpu.VMEM((tall + 1, TILE, wide), F32)],
        ),
        out_shape=jax.ShapeDtypeStruct((tall, TILE, wide), BF),
        name="build_block",
    )(live_count, row_ids, col_ids, weights_all)


class Place:
    def __init__(self):
        row = lax.axis_index("row")
        col = lax.axis_index("col")
        self.row, self.col = row, col
        self.x, self.low = row // 2, row % 2
        self.high, self.z, self.core = col // 16, (col // 2) % 8, col % 2
        self.y = self.high * 2 + self.low

    def at(self, x=None, y=None, z=None, core=None):
        x = self.x if x is None else x
        y = self.y if y is None else y
        z = self.z if z is None else z
        core = self.core if core is None else core
        return (x * 2 + y % 2, (y // 2) * 16 + z * 2 + core)

    def along(self, axis, offset):
        size = {"x": 4, "y": 4, "z": 8}[axis]
        return self.at(**{axis: (getattr(self, axis) + offset + size) % size})


class Wire:
    def __init__(self, send, recv):
        self.send, self.recv, self.copies = send, recv, []

    def push(self, source, target, device):
        index = len(self.copies)
        copy = pltpu.make_async_remote_copy(
            src_ref=source,
            dst_ref=target,
            send_sem=self.send.at[index],
            recv_sem=self.recv.at[index],
            device_id=device,
            device_id_type=MESH,
        )
        copy.start()
        self.copies.append([copy, False])
        return index

    def arrived(self, index):
        if not self.copies[index][1]:
            self.copies[index][0].wait_recv()
            self.copies[index][1] = True

    def finish(self):
        for index, (copy, _) in enumerate(self.copies):
            self.arrived(index)
            copy.wait_send()


def enter(devices):
    barrier = pltpu.get_barrier_semaphore()
    for device in devices:
        pl.semaphore_signal(barrier, inc=1, device_id=device, device_id_type=MESH)
    pl.semaphore_wait(barrier, len(devices))


def halves(size):
    return (pl.ds(0, size // 2), pl.ds(size // 2, size // 2))


def contract(a, b, left, right):
    return lax.dot_general(a, b, (((left,), (right,)), ((), ())), preferred_element_type=F32)


def layer_body(
    factor,
    features, adjacency, cot, kinds, table, w_in, w_out,
    mixed, grad_x, w_all, gain,
    sources, blocks, own, sib_out, sib_in, z_out, z_in, y_out, y_in,
    mine, gathered, back, grad_act, gains,
    scaled2, act_half, act2, hid_half, hid2, cot2,
    weights, x_out, x_in, summed, v_out, v_in, w_part, w_in_z, piece, g_out, g_in,
    b_out, b_in, c_out, c_in,
    local, send, recv,
):
    me, wire = Place(), Wire(send, recv)
    twin = me.at(core=1 - me.core)
    across = me.along("y", 2)
    mate = me.at(y=me.high * 2 + 1 - me.low)
    z_side = (me.along("z", 1), me.along("z", -1))
    x_side = (me.along("x", 1), me.along("x", -1))
    y_side = (me.along("y", 1), me.along("y", -1))
    z_all = [me.along("z", step) for step in range(1, 8)]
    whole = pl.ds(0, TILE)

    loads = []
    for order, offset in enumerate(OFFSETS):
        group = []
        for part in range(4):
            which, side = part // 2, part % 2
            high = (me.high + 1 + side) % 2
            core = me.core if which == 0 else 1 - me.core
            tile = high * 16 + ((me.z + offset) % 8) * 2 + core
            copy = pltpu.make_async_copy(
                adjacency.at[tile],
                blocks.at[order, pl.ds(part * TILE, TILE)],
                local.at[order * 4 + part],
            )
            copy.start()
            group.append(copy)
        loads.append(group)

    enter([twin, across, *z_side, *x_side, *y_side])

    row = me.row
    first = wire.push(features, sources.at[row], mate)
    direct = [wire.push(features, sources.at[row], device) for device in x_side]
    cot_sent = wire.push(cot, cot2.at[pl.ds(TILE, TILE)], twin)
    sources[row] = features[...]
    wire.arrived(first)
    row_mate = me.x * 2 + 1 - me.low
    other = [wire.push(sources.at[row_mate], sources.at[row_mate], device) for device in x_side]
    cot2[0:TILE] = cot[...]
    grad_act[...] = contract(cot[...], w_out[...], 1, 1)
    kind = jnp.transpose(jnp.broadcast_to(kinds[...].astype(F32), (TILE, TILE)))[:, :1]
    chosen = jnp.zeros((TILE, F), F32)
    for t in range(TYPES):
        chosen = jnp.where(kind == float(t), table[t : t + 1], chosen)
    gains[...] = chosen
    for pair, low in ((direct, me.low), (other, 1 - me.low)):
        for turn, rows in enumerate(halves(TILE)):
            wire.arrived(pair[turn])
            held = ((me.x + (3 if turn == 0 else 1)) % 4) * 2 + low
            view = sources.at[held, rows]
            pair[turn] = wire.push(view, view, x_side[turn])
    for pair in (direct, other):
        for turn in range(2):
            wire.arrived(pair[turn])

    parts = {}

    def multiply(order):
        for copy in loads[order]:
            copy.wait()
        value = sources[...].reshape(sources.shape[0] * TILE, F)
        sib_out[order] = contract(blocks[order, 256:512], value, 1, 0)
        parts[order] = wire.push(sib_out.at[order], sib_in.at[order], twin)
        own[order] = contract(blocks[order, 0:256], value, 1, 0)

    sent = {}

    def reduce_hop(hop):
        for side in range(2):
            for turn in range(2):
                order = OFFSETS.index(hop if turn == 0 else 8 - hop)
                wire.arrived(parts[order])
                for part in range(2):
                    if hop == 4 and part != turn:
                        continue
                    rows = pl.ds(part * 64, 64)
                    base = pl.ds(side * TILE + part * 64, 64)
                    value = own[order, base] + sib_in[order, base]
                    if hop < 3 or (hop == 3 and part == turn):
                        wire.arrived(sent[turn, side, hop + 1])
                        value = value + z_in[turn, side, hop, rows].astype(F32)
                    z_out[turn, side, hop - 1, rows] = value.astype(BF)
                moved = pl.ds(turn * 64, 64) if hop == 4 else whole
                sent[turn, side, hop] = wire.push(
                    z_out.at[turn, side, hop - 1, moved],
                    z_in.at[turn, side, hop - 1, moved],
                    z_side[turn],
                )

    multiply(0)
    multiply(1)
    reduce_hop(4)
    multiply(2)
    reduce_hop(3)
    multiply(3)
    multiply(4)
    reduce_hop(2)
    multiply(5)
    multiply(6)
    reduce_hop(1)
    multiply(7)
    wire.arrived(parts[7])
    ends = []
    for side in range(2):
        rows = pl.ds(side * TILE, TILE)
        value = own[7, rows] + sib_in[7, rows]
        for turn in range(2):
            wire.arrived(sent[turn, side, 1])
            value = value + z_in[turn, side, 0].astype(F32)
        if side == 0:
            y_out[...] = value.astype(BF)
            crossed = wire.push(y_out, y_in, across)
        else:
            ends.append(value)
    wire.arrived(crossed)
    aggregate = ends[0] + y_in[...].astype(F32)

    center = jnp.mean(aggregate, axis=-1, keepdims=True)
    spread = jnp.mean(jnp.square(aggregate - center), axis=-1, keepdims=True)
    inverse = lax.rsqrt(spread + 1e-05)
    normed = (aggregate - center) * inverse
    scaled = (normed * gains[...]).astype(BF)
    scaled2[0:TILE] = scaled
    late = pl.ds(TILE, TILE)
    scaled_sent = wire.push(scaled2.at[whole], scaled2.at[late], twin)
    hidden = contract(scaled, w_in[...], 1, 0)
    sigmoid = jax.nn.sigmoid(hidden)
    activated = (hidden * sigmoid).astype(BF)
    grad_hidden = (grad_act[...] * sigmoid * (1.0 + hidden * (1.0 - sigmoid))).astype(BF)
    grad_scaled = contract(grad_hidden, w_in[...], 1, 1)
    grad_normed = grad_scaled * gains[...]
    grad_rows = cot[...].astype(F32) + inverse * (
        grad_normed
        - jnp.mean(grad_normed, axis=-1, keepdims=True)
        - normed * jnp.mean(grad_normed * normed, axis=-1, keepdims=True)
    )
    turned = jnp.transpose(grad_rows).astype(BF)
    mine[...] = turned
    col = me.col
    crossed = wire.push(mine, gathered.at[col], across)
    own_sent = [wire.push(mine, gathered.at[col], device) for device in z_side]
    shared = {(0, 0): wire.push(mine, gathered.at[col], twin)}
    gathered[col] = turned
    for half in range(2):
        act_half[half] = activated[:, half * F : (half + 1) * F]
        hid_half[half] = grad_hidden[:, half * F : (half + 1) * F]
    act_sent = wire.push(act_half.at[1 - me.core], act2.at[late], twin)
    hid_sent = wire.push(hid_half.at[1 - me.core], hid2.at[late], twin)
    act2[0:TILE] = act_half[me.core]
    hid2[0:TILE] = hid_half[me.core]
    product = grad_scaled * normed
    for t in range(TYPES):
        g_out[0, t : t + 1] = jnp.sum(
            jnp.where(kind == float(t), product, 0.0), axis=0, keepdims=True
        )
    tally = {"sent": wire.push(g_out.at[0], g_in.at[0], twin), "phase": 0}

    def gain_step(device):
        phase = tally["phase"]
        wire.arrived(tally["sent"])
        g_out[phase + 1] = g_out[phase] + g_in[phase]
        tally["sent"] = wire.push(g_out.at[phase + 1], g_in.at[phase + 1], device)
        tally["phase"] = phase + 1

    def index_of(family, offset, core):
        high = me.high if family == 0 else 1 - me.high
        return high * 16 + ((me.z + offset + 8) % 8) * 2 + core

    flows = [own_sent, None]

    def forward(hop, family):
        for turn in range(2):
            wire.arrived(flows[family][turn])
            offset = 1 - hop if turn == 0 else hop - 1
            place = index_of(family, offset, me.core)
            moved = halves(F)[turn] if hop == 4 else pl.ds(0, F)
            view = gathered.at[place, moved]
            flows[family][turn] = wire.push(view, view, z_side[turn])
            view = gathered.at[place]
            shared[family, offset % 8] = wire.push(view, view, twin)

    def pull(offset):
        order = OFFSETS.index(offset)
        pieces = []
        for part in range(4):
            which, side = part // 2, part % 2
            if which == 1:
                wire.arrived(shared[1 - side, offset])
            core = me.core if which == 0 else 1 - me.core
            pieces.append(gathered[index_of(1 - side, offset, core)])
        value = contract(jnp.concatenate(pieces, axis=1), blocks[order], 1, 0)
        for part in range(8):
            piece_of = value[:, part * TILE : (part + 1) * TILE]
            back[part] = piece_of if offset == 0 else back[part] + piece_of

    ring = {}

    def weight_start():
        for arrival in (cot_sent, scaled_sent, act_sent, hid_sent):
            wire.arrived(arrival)
        far = (me.x + 2) % 4
        for part in range(4):
            columns = slice((part % 2) * 256, (part % 2) * 256 + 256)
            if part < 2:
                weights[part] = contract(act2[:, columns], cot2[...], 0, 0)
            else:
                weights[part] = contract(scaled2[:, columns], hid2[...], 0, 0)
        for turn, rows in enumerate(halves(256)):
            x_out[turn, 1, rows] = weights[far, rows].astype(BF)
            ring[turn] = wire.push(x_out.at[turn, 1, rows], x_in.at[turn, 1, rows], x_side[turn])

    def weight_x():
        for turn, rows in enumerate(halves(256)):
            rest = halves(256)[1 - turn]
            near = (me.x + (1 if turn == 0 else 3)) % 4
            wire.arrived(ring[turn])
            x_out[turn, 0, rest] = weights[near, rest].astype(BF)
            x_out[turn, 0, rows] = (
                weights[near, rows] + x_in[turn, 1, rows].astype(F32)
            ).astype(BF)
            ring[turn] = wire.push(x_out.at[turn, 0], x_in.at[turn, 0], x_side[turn])

    def weight_y_start():
        for turn in range(2):
            wire.arrived(ring[turn])
        for part in range(4):
            rows = pl.ds(part * 64, 64)
            summed[part] = (
                weights[me.x, rows] + x_in[0, 0, rows].astype(F32) + x_in[1, 0, rows].astype(F32)
            )
        far = (me.y + 2) % 4
        for turn, rows in enumerate(halves(64)):
            v_out[turn, 1, rows] = summed[far, rows]
            ring[turn] = wire.push(v_out.at[turn, 1, rows], v_in.at[turn, 1, rows], y_side[turn])

    def weight_y():
        for turn, rows in enumerate(halves(64)):
            rest = halves(64)[1 - turn]
            near = (me.y + (1 if turn == 0 else 3)) % 4
            wire.arrived(ring[turn])
            v_out[turn, 0, rest] = summed[near, rest]
            v_out[turn, 0, rows] = summed[near, rows] + v_in[turn, 1, rows]
            ring[turn] = wire.push(v_out.at[turn, 0], v_in.at[turn, 0], y_side[turn])

    def weight_z_start():
        for turn in range(2):
            wire.arrived(ring[turn])
        for part in range(8):
            rows = pl.ds(part * 8, 8)
            w_part[part] = summed[me.y, rows] + v_in[0, 0, rows] + v_in[1, 0, rows]
        ring["z"] = [
            wire.push(w_part.at[(me.z + step) % 8], w_in_z.at[step - 1], z_all[step - 1])
            for step in range(1, 8)
        ]

    def weight_z():
        total = w_part[me.z]
        for step in range(7):
            wire.arrived(ring["z"][step])
            total = total + w_in_z[step]
        total = (total * factor).astype(BF)
        piece[...] = total
        w_all[me.core, me.x, me.y, me.z] = total
        spot = w_all.at[me.core, me.x, me.y, me.z]
        ring["z"] = [wire.push(piece, spot, device) for device in z_all]

    def spread_y():
        for index in ring["z"]:
            wire.arrived(index)
        view = w_all.at[me.core, me.x, me.y]
        ring["y"] = [wire.push(view, view, device) for device in y_side]

    def spread_y_far():
        for turn in range(2):
            wire.arrived(ring["y"][turn])
            held = (me.y + (3 if turn == 0 else 1)) % 4
            view = w_all.at[me.core, me.x, held, pl.ds(turn * 4, 4)]
            ring["y"][turn] = wire.push(view, view, y_side[turn])

    def spread_x():
        for turn in range(2):
            wire.arrived(ring["y"][turn])
        view = w_all.at[me.core, me.x]
        ring["x"] = [wire.push(view, view, device) for device in x_side]
        wire.push(view, view, twin)

    def spread_x_far():
        for turn in range(2):
            wire.arrived(ring["x"][turn])
            held = (me.x + (3 if turn == 0 else 1)) % 4
            view = w_all.at[me.core, held, pl.ds(turn * 2, 2)]
            ring["x"][turn] = wire.push(view, view, x_side[turn])
            view = w_all.at[me.core, held]
            wire.push(view, view, twin)

    wire.arrived(crossed)
    place = index_of(1, 0, me.core)
    view = gathered.at[place]
    flows[1] = [wire.push(view, view, device) for device in z_side]
    shared[1, 0] = wire.push(view, view, twin)
    mixed[...] = (aggregate + contract(activated, w_out[...], 1, 0)).astype(BF)
    forward(2, 0)
    weight_start()
    forward(2, 1)
    gain_step(me.at(x=me.x + 1 - 2 * (me.x % 2)))
    pull(0)
    forward(3, 0)
    pull(7)
    forward(3, 1)
    weight_x()
    gain_step(me.at(x=3 - me.x))
    pull(1)
    forward(4, 0)
    pull(6)
    forward(4, 1)
    weight_y_start()
    gain_step(me.at(y=me.y + 1 - 2 * (me.y % 2)))
    pull(2)
    weight_y()
    gain_step(me.at(y=3 - me.y))
    for family in range(2):
        for turn in range(2):
            wire.arrived(flows[family][turn])
        view = gathered.at[index_of(family, 4, me.core)]
        shared[family, 4] = wire.push(view, view, twin)
    pull(5)
    weight_z_start()
    gain_step(me.at(z=me.z + 1 - 2 * (me.z % 2)))
    pull(3)
    pull(4)

    flow = {}
    for side in range(2):
        low = (me.low + 1 + side) % 2
        far = ((me.x + 2) % 4) * 2 + low
        for turn, rows in enumerate(halves(F)):
            b_out[turn, side, 1, rows] = back[far, rows].astype(BF)
            flow[turn, side] = wire.push(
                b_out.at[turn, side, 1, rows], b_in.at[turn, side, 1, rows], x_side[turn]
            )
    weight_z()
    gain_step(me.at(z=(me.z // 4) * 4 + 3 - me.z % 4))
    for side in range(2):
        low = (me.low + 1 + side) % 2
        for turn, rows in enumerate(halves(F)):
            wire.arrived(flow[turn, side])
            near = ((me.x + (1 if turn == 0 else 3)) % 4) * 2 + low
            rest = halves(F)[1 - turn]
            b_out[turn, side, 0, rest] = back[near, rest].astype(BF)
            b_out[turn, side, 0, rows] = (
                back[near, rows] + b_in[turn, side, 1, rows].astype(F32)
            ).astype(BF)
            flow[turn, side] = wire.push(
                b_out.at[turn, side, 0], b_in.at[turn, side, 0], x_side[turn]
            )
    spread_y()
    gain_step(me.at(z=(me.z + 4) % 8))
    spread_y_far()
    spread_x()
    ends = []
    for side in range(2):
        low = (me.low + 1 + side) % 2
        value = back[me.x * 2 + low]
        for turn in range(2):
            wire.arrived(flow[turn, side])
            value = value + b_in[turn, side, 0].astype(F32)
        if side == 0:
            c_out[...] = value.astype(BF)
            crossed = wire.push(c_out, c_in, mate)
        else:
            ends.append(value)
    spread_x_far()
    wire.arrived(crossed)
    grad_x[...] = jnp.transpose(ends[0] + c_in[...].astype(F32))
    phase = tally["phase"]
    wire.arrived(tally["sent"])
    gain[...] = (g_out[phase] + g_in[phase]) * factor
    for turn in range(2):
        wire.arrived(ring["x"][turn])
    view = w_all.at[me.core, (me.x + 2) % 4]
    wire.push(view, view, twin)
    wire.finish()


def unpack_body(w_all, mixed, grad_x, gain, out_mixed, out_x, out_in, out_out, out_gain):
    for core in range(2):
        for part in range(4):
            value = w_all[core, part].astype(F32).reshape(256, F)
            if part < 2:
                out_out[core * F + part * 256 : core * F + part * 256 + 256] = value
            else:
                rows = slice((part - 2) * 256, (part - 2) * 256 + 256)
                out_in[rows, core * F : (core + 1) * F] = value
    out_mixed[...] = mixed[...]
    out_x[...] = grad_x[...]
    out_gain[...] = gain[...]


def shards(
    features,
    tile_vals,
    tile_row,
    tile_col,
    tile_count,
    node_type,
    type_gain,
    w_in,
    w_out,
    cotangent,
):
    row_count = lax.axis_size("row")
    col_count = lax.axis_size("col")
    hid = w_in.shape[1]
    factor = float(TILE * row_count * col_count) ** (-0.5)
    shape = jax.ShapeDtypeStruct
    vmem = pltpu.VMEM
    wide = row_count * TILE
    adjacency = build(tile_vals[0], tile_row[0], tile_col[0], tile_count[0], col_count, wide)
    space = lambda kind: pl.BlockSpec(memory_space=kind)
    copies = 128
    mixed, grad_x, w_all, gain = pl.pallas_call(
        functools.partial(layer_body, factor),
        out_shape=[
            shape((TILE, F), BF),
            shape((TILE, F), F32),
            shape((2, 4, 4, 8, 8, F), BF),
            shape((TYPES, F), F32),
        ],
        in_specs=[space(vmem), space(pl.ANY)] + [space(vmem)] * 5,
        out_specs=[space(vmem)] * 4,
        scratch_shapes=[
            vmem((row_count, TILE, F), BF),
            vmem((8, 4 * TILE, wide), BF),
            vmem((8, 2 * TILE, F), F32), vmem((8, 2 * TILE, F), F32), vmem((8, 2 * TILE, F), F32),
            vmem((2, 2, 4, TILE, F), BF), vmem((2, 2, 4, TILE, F), BF),
            vmem((TILE, F), BF), vmem((TILE, F), BF),
            vmem((F, TILE), BF), vmem((col_count, F, TILE), BF), vmem((row_count, F, TILE), F32),
            vmem((TILE, hid), F32), vmem((TILE, F), F32),
            vmem((2 * TILE, F), BF), vmem((2, TILE, F), BF), vmem((2 * TILE, F), BF),
            vmem((2, TILE, F), BF), vmem((2 * TILE, F), BF), vmem((2 * TILE, F), BF),
            vmem((4, 256, F), F32), vmem((2, 2, 256, F), BF), vmem((2, 2, 256, F), BF),
            vmem((4, 64, F), F32), vmem((2, 2, 64, F), F32), vmem((2, 2, 64, F), F32),
            vmem((8, 8, F), F32), vmem((7, 8, F), F32), vmem((8, F), BF),
            vmem((8, TYPES, F), F32), vmem((8, TYPES, F), F32),
            vmem((2, 2, 2, F, TILE), BF), vmem((2, 2, 2, F, TILE), BF),
            vmem((F, TILE), BF), vmem((F, TILE), BF),
            pltpu.SemaphoreType.DMA((32,)),
            pltpu.SemaphoreType.DMA((copies,)), pltpu.SemaphoreType.DMA((copies,)),
        ],
        compiler_params=pltpu.CompilerParams(
            collective_id=1, has_side_effects=True, vmem_limit_bytes=60 * 2**20
        ),
        name="layer",
    )(features, adjacency, cotangent, node_type[None, :], type_gain, w_in, w_out)
    mixed, grad_x, grad_w_in, grad_w_out, gain = pl.pallas_call(
        unpack_body,
        out_shape=[
            shape((TILE, F), BF), shape((TILE, F), F32), shape((F, hid), F32),
            shape((hid, F), F32), shape((TYPES, F), F32),
        ],
        name="unpack",
    )(w_all, mixed, grad_x, gain)
    return (mixed, grad_x, grad_w_in, grad_w_out, gain)


def solution(mesh):
    return jax.shard_map(
        shards,
        mesh=mesh,
        in_specs=(
            P(("col", "row"), None),
            P("row", "col", None, None),
            P("row", "col"),
            P("row", "col"),
            P("row", "col"),
            P(("row", "col")),
            P(),
            P(),
            P(),
            P(("row", "col"), None),
        ),
        out_specs=(P(("row", "col"), None), P(("col", "row"), None), P(), P(), P()),
        check_vma=False,
    )
```

time: 773 us -> 133 us (0.17)
  waiting for transfers between devices: 394 us -> 0 us
  other arithmetic: 147 us -> 0 us
  Pallas kernels: 0 us -> 132 us
  matrix products: 76.7 us -> 0 us
  blocking collectives: 75.5 us -> 0 us
  local copies, waits for them, and re-layouts: 61.3 us -> 0 us
  between operations: 13.9 us -> 1.29 us
    reduce_scatter x2 -> x0, waiting for transfers between devices: 207 us -> none  [the longest x1 156 us: shards(): lax.psum_scatter(totals.reshape(col_count * TILE, F), 'col', scatter_dime...]
    pallas_call x0 -> x3, Pallas kernels: none -> 132 us  [the longest x1 119 us: shards(): pl.pallas_call(functools.partial(layer_body, factor), out_shape=[shape((T...]
    scatter-add x16 -> x0, other arithmetic: 126 us -> none  [advance(): return totals.at[placed].add(product)]
    all_gather x2 -> x0, waiting for transfers between devices: 121 us -> none  [the longest x1 79.1 us: shards(): lax.all_gather(grad_rows, 'col', axis=0, tiled=True)]
    dot_general x24 -> x0, matrix products: 76.7 us -> none  [the longest x8 35.3 us: advance(): jnp.einsum('sab,saf->sbf', weights_now, pieces, preferred_element_type=jn...]
    psum x1 -> x0, blocking collectives: 75.5 us -> none  [shards(): reduced = lax.psum((grad_in_w, grad_out_w, grad_gain), ('row', 'col'))]
    psum x1 -> x0, waiting for transfers between devices: 65.1 us -> none  [shards(): reduced = lax.psum((grad_in_w, grad_out_w, grad_gain), ('row', 'col'))]
    gather x16 -> x0, local copies, waits for them, and re-layouts: 49 us -> none  [the longest x8 33.8 us: advance(): pieces = sources[row_ids]]
  transfers between devices with their start and end apart: 5 -> 0, of which waited for: 5 -> 0; matrix products, arithmetic and copies ran while one was open for 19% -> 0% of each run, Pallas kernels for 0% -> 0%
where the time goes in v2:
time: 133 us
  Pallas kernels  132 us (99%)
    pallas_call x1, Pallas kernels, shards(): pl.pallas_call(functools.partial(layer_body, factor), out_shape=[shape((T...  119 us
    pallas_call x1, Pallas kernels, build(): pl.pallas_call(build_body, grid_spec=pltpu.PrefetchScalarGridSpec(num_sca...  8.13 us
    pallas_call x1, Pallas kernels, shards(): pl.pallas_call(unpack_body, out_shape=[shape((TILE, F), BF), shape((TILE,...  3.95 us

profile of v2, /device:TPU:1, one launch (start us, length us, event | category | flops | bytes accessed | tf_op | source)
XLA Modules:
  0.0 132.8 jit_solution(13596375820733882064)
XLA Ops:
  1.3 8.1 %build_block.1.adjacency = bf16[32,128,1024]{2,1,0:T(8,128)(2,1)} custom-call(s32[1]{0:T(128)} %bitcast.5.count, s32[128]{0:T(128)} %bitcast.7, s32[128]{0:T(128)} %bitcast.8, bf16[128,128,128]{2,1,0:T(8,128)(2,1)} %bitcast.6), custom_call_target="tpu_custom_call" | custom-call | tf_op jit(solution)/shard_map/build_block/pallas_call | solution.py:53
  9.4 119.4 %layer.1 = (bf16[128,512]{1,0:T(8,128)(2,1)}, f32[128,512]{1,0:T(8,128)}, bf16[2,4,4,8,8,512]{5,4,3,2,1,0:T(8,128)(2,1)}, f32[8,512]{1,0:T(8,128)}) custom-call(bf16[128,512]{1,0:T(8,128)(2,1)} %features.1, bf16[32,128,1024]{2,1,0:T(8,128)(2,1)} %build_block.1.adjacency, bf16[128,512]{1,0:T(8,128)(2,1)} %cot.1, s32[1,128]{1,0:T(1,128)} %bitcast.9, ...), custom_call_target="tpu_custom_call" | custom-call | tf_op jit(solution)/shard_map/layer/pallas_call | solution.py:568
  128.8 4.0 %unpack.1 = (bf16[128,512]{1,0:T(8,128)(2,1)}, f32[128,512]{1,0:T(8,128)}, f32[512,1024]{1,0:T(8,128)}, f32[1024,512]{1,0:T(8,128)}, f32[8,512]{1,0:T(8,128)}) custom-call(bf16[2,4,4,8,8,512]{5,4,3,2,1,0:T(8,128)(2,1)} %get-tuple-element.9.w_all, bf16[128,512]{1,0:T(8,128)(2,1)} %get-tuple-element.10.mixed, f32[128,512]{1,0:T(8,128)} %get-tuple-element.11.grad_x, ...), custom_call_target="tpu_custom_call" | custom-call | tf_op jit(solution)/shard_map/unpack/pallas_call | solution.py:602
